TPU v7x, 256 devices: a whole 4x4x8 slice. The times are simulated.
256 devices in a mesh: facet: 8 (over x_hi, y), tm: 32 (over z, x_lo, core).
Axes of the slice: x: 4 (x_hi: 2, x_lo: 2; x = x_hi * 2 + x_lo), y: 4, z: 8, core: 2. Of those that a mesh axis runs over, the one named last changes fastest.
Arguments:
- visibilities: bfloat16 [2, 4096, 128], P(None, ('tm', 'facet')), may hold values from -6 to 6
- coordinates: bfloat16 [3, 4096, 128], P(None, ('tm', 'facet')), may hold values from -12 to 12
- station_screens: bfloat16 [2, 512, 2, 1024], P(None, 'tm'), may hold values from -5 to 5
- subgrid_stations: int32 [4096, 2], P('tm'), may hold values from 0 to 511, as said below
- subgrid_corners: int32 [4096, 2], P('tm'), may hold values from -32768 to 32736
- facet_member: int32 [4096, 8], P('tm', 'facet'), may hold values 0 or 1
Outputs:
- facets: float32 [2, 8, 512, 512], P(None, 'facet', 'tm')
Inputs may be any that keep to these rules, and one draw needn't show every extreme that they name: `subgrid_stations`: the two stations of a subgrid differ.
All inputs are finite; a program needn't handle non-finite values. No bound on the sum of `facet_member` on one device may be relied on, other than what follows from the above.
Results may differ from a plain program's by a relative error of at most 0.013.
Values may be sent and summed in bfloat16 or wider, within the bound.
A program may use at most 64 MiB of HBM per device.

v0:
```python
import functools
import math

import jax
import jax.numpy as jnp
import numpy as np
from jax import lax
from jax.experimental import pallas as pl
from jax.experimental.pallas import tpu as pltpu
from jax.sharding import PartitionSpec as P

GRID = 65536
S = 32
NT = 128
SLABS = 2
FP = 512
LANES = 128
GROUPS = 8
RADIX = 4
MESH = pl.DeviceIdType.MESH
F32 = jnp.float32
BF16 = jnp.bfloat16


def rounded(values):
    return np.asarray(values, np.float32).astype(jnp.bfloat16)


def complex_block(values):
    return np.block([[values.real, values.imag], [-values.imag, values.real]])


def dft_rows_table():
    offsets = np.arange(S) - S // 2
    table = np.exp(-2j * np.pi * (np.outer(offsets, offsets) % S) / S) / math.sqrt(S)
    return rounded(complex_block(np.kron(np.eye(RADIX), table.T)))


def dft_columns_table():
    tables = []
    for a_lo in range(GROUPS):
        offset = 8 * (np.arange(RADIX) - 2) + a_lo
        factor = (-1.0) ** a_lo * np.exp(-2j * np.pi * np.outer(np.arange(RADIX), offset) / S) / math.sqrt(S)
        tables.append(rounded(complex_block(np.kron(factor, np.eye(S)))))
    return np.stack(tables)


def facet_table():
    angles = 2.0 * np.pi * (np.outer(np.arange(FP), np.arange(FP)) % FP) / FP
    return rounded(np.concatenate([np.cos(angles), np.sin(angles)], axis=1))


def taper_table():
    centre = np.sin(np.pi * (np.arange(S) + 0.5) / S)
    return np.outer(centre, centre).reshape(GROUPS, LANES).astype(np.float32)


def cos_sin(turns):
    rest = turns - jnp.round(turns)
    angle = rest * math.pi
    square = angle * angle
    sin_half = -1.0 / 39916800.0
    for term in (1.0 / 362880.0, -1.0 / 5040.0, 1.0 / 120.0, -1.0 / 6.0, 1.0):
        sin_half = sin_half * square + term
    sin_half = sin_half * angle
    cos_half = 1.0 / 479001600.0
    for term in (-1.0 / 3628800.0, 1.0 / 40320.0, -1.0 / 720.0, 1.0 / 24.0, -0.5, 1.0):
        cos_half = cos_half * square + term
    return 1.0 - 2.0 * sin_half * sin_half, 2.0 * sin_half * cos_half


def dot(left, right):
    return jnp.dot(left, right, preferred_element_type=F32)


def own_images(inputs_ref, image_ref):
    row = lax.broadcasted_iota(jnp.int32, (S, NT), 0)
    cell_left = (RADIX * (row % GROUPS) + row // GROUPS - S // 2).astype(F32) / S
    cell_right = (row - S // 2).astype(F32) / S
    half_left = cell_left * cell_left * 0.5
    half_right = cell_right * cell_right * 0.5
    lane_block = lax.broadcasted_iota(jnp.int32, (GROUPS, LANES), 1) // S

    def one(number, carry):
        vis_real, vis_imag, shift_u, shift_v, shift_w = (
            inputs_ref[part, pl.ds(number, 1), :] for part in range(5)
        )
        cos_left, sin_left = cos_sin(shift_u * cell_left - shift_w * half_left)
        cos_right, sin_right = cos_sin(shift_v * cell_right - shift_w * half_right)
        left = jnp.concatenate(
            [vis_real * cos_left - vis_imag * sin_left, vis_real * sin_left + vis_imag * cos_left], axis=0
        ).astype(BF16)
        right = jnp.concatenate([cos_right] * RADIX + [sin_right] * RADIX, axis=0).astype(BF16)
        product = lax.dot_general(left, right, (((1,), (1,)), ((), ())), preferred_element_type=F32)
        real = product[:S, :LANES] - product[S:, LANES:]
        imag = product[:S, LANES:] + product[S:, :LANES]
        for part, whole in ((0, real), (1, imag)):
            chosen = whole[:GROUPS]
            for block in range(1, RADIX):
                chosen = jnp.where(lane_block == block, whole[GROUPS * block : GROUPS * (block + 1)], chosen)
            for block in range(GROUPS):
                image_ref[block, part, pl.ds(number, 1), :] = chosen[block : block + 1]
        return carry

    lax.fori_loop(0, inputs_ref.shape[1], one, 0)


def rows_kernel(
    facets,
    times,
    vis_ref,
    coord_ref,
    screen_ref,
    station_ref,
    taper_ref,
    table_ref,
    out_ref,
    inputs,
    image,
    images,
    screens,
    mixed,
    image_send,
    image_recv,
    screen_send,
    screen_recv,
    out_send,
    out_recv,
):
    facet = lax.axis_index("facet")
    time = lax.axis_index("tm")
    barrier = pltpu.get_barrier_semaphore()
    for step in range(1, facets):
        pl.semaphore_signal(
            barrier, inc=1, device_id={"facet": lax.rem(facet + step, facets)}, device_id_type=MESH
        )
    for step in range(1, times):
        pl.semaphore_signal(barrier, inc=1, device_id={"tm": lax.rem(time + step, times)}, device_id_type=MESH)

    inputs[0:2] = vis_ref[...].astype(F32)
    inputs[2:5] = coord_ref[...].astype(F32)
    pl.semaphore_wait(barrier, facets - 1 + times - 1)

    screen_copies = []
    for step in range(1, times):
        target = lax.rem(time + step, times)
        copy = pltpu.make_async_remote_copy(
            src_ref=screen_ref.at[target // (times // SLABS)],
            dst_ref=screens.at[time],
            send_sem=screen_send.at[step],
            recv_sem=screen_recv.at[step],
            device_id={"tm": target},
            device_id_type=MESH,
        )
        copy.start()
        screen_copies.append(copy)
    screens[time] = screen_ref[time // (times // SLABS)]

    own_images(inputs, image)

    image_copies = []
    for step in range(1, facets):
        target = lax.rem(facet + step, facets)
        copy = pltpu.make_async_remote_copy(
            src_ref=image.at[target],
            dst_ref=images.at[facet],
            send_sem=image_send.at[step],
            recv_sem=image_recv.at[step],
            device_id={"facet": target},
            device_id_type=MESH,
        )
        copy.start()
        image_copies.append(copy)
    images[facet] = image[facet]
    for copy in image_copies + screen_copies:
        copy.wait()

    count = station_ref.shape[0]
    stations = screens.shape[0] * screens.shape[2]
    screen_pair = jnp.concatenate(
        [screens[:, 0].reshape(stations, LANES), screens[:, 1].reshape(stations, LANES)], axis=1
    )
    station = lax.broadcasted_iota(jnp.int32, (count, stations), 1)
    first = dot((station == station_ref[:, 0:1]).astype(F32).astype(BF16), screen_pair)
    second = dot((station == station_ref[:, 1:2]).astype(F32).astype(BF16), screen_pair)
    first_real, first_imag = first[:, :LANES], first[:, LANES:]
    second_real, second_imag = second[:, :LANES], second[:, LANES:]
    taper = taper_ref[pl.ds(facet, 1), :]
    weight_real = taper * (first_real * second_real + first_imag * second_imag)
    weight_imag = taper * (first_real * second_imag - first_imag * second_real)
    image_real = images[:, 0].reshape(count, LANES)
    image_imag = images[:, 1].reshape(count, LANES)
    weighted = jnp.concatenate(
        [
            weight_real * image_real - weight_imag * image_imag,
            weight_real * image_imag + weight_imag * image_real,
        ],
        axis=1,
    ).astype(BF16)
    mixed[...] = dot(weighted, table_ref[...]).astype(BF16)

    out_copies = []
    for step in range(1, facets):
        copy = pltpu.make_async_remote_copy(
            src_ref=mixed,
            dst_ref=out_ref.at[facet],
            send_sem=out_send.at[step],
            recv_sem=out_recv.at[step],
            device_id={"facet": lax.rem(facet + step, facets)},
            device_id_type=MESH,
        )
        copy.start()
        out_copies.append(copy)
    out_ref[facet] = mixed[...]
    for copy in out_copies:
        copy.wait()


def gather_rows(visibilities, coordinates, screens, stations, facets, times):
    own = visibilities.shape[1]
    count = stations.shape[0]
    vmem = pl.BlockSpec(memory_space=pltpu.VMEM)
    return pl.pallas_call(
        functools.partial(rows_kernel, facets, times),
        out_shape=jax.ShapeDtypeStruct((facets, count, 2 * LANES), BF16),
        in_specs=[vmem] * 6,
        out_specs=vmem,
        scratch_shapes=[
            pltpu.VMEM((5, own, NT), F32),
            pltpu.VMEM((GROUPS, 2, own, LANES), F32),
            pltpu.VMEM((GROUPS, 2, own, LANES), F32),
            pltpu.VMEM((times,) + screens.shape[1:], BF16),
            pltpu.VMEM((count, 2 * LANES), BF16),
            pltpu.SemaphoreType.DMA((facets,)),
            pltpu.SemaphoreType.DMA((facets,)),
            pltpu.SemaphoreType.DMA((times,)),
            pltpu.SemaphoreType.DMA((times,)),
            pltpu.SemaphoreType.DMA((facets,)),
            pltpu.SemaphoreType.DMA((facets,)),
        ],
        compiler_params=pltpu.CompilerParams(collective_id=0, has_side_effects=True),
        name="subgrid_rows",
    )(
        visibilities,
        coordinates,
        screens,
        stations,
        jnp.asarray(taper_table()),
        jnp.asarray(dft_rows_table()),
    )


def eight_point(parts):
    root = math.sqrt(0.5)

    def add(a, b):
        return a[0] + b[0], a[1] + b[1]

    def sub(a, b):
        return a[0] - b[0], a[1] - b[1]

    def minus_i(a):
        return a[1], -a[0]

    def four_point(p):
        even_sum, even_diff = add(p[0], p[2]), sub(p[0], p[2])
        odd_sum, odd_diff = add(p[1], p[3]), minus_i(sub(p[1], p[3]))
        return add(even_sum, odd_sum), add(even_diff, odd_diff), sub(even_sum, odd_sum), sub(even_diff, odd_diff)

    even = four_point(parts[0::2])
    odd = list(four_point(parts[1::2]))
    odd[1] = ((odd[1][0] + odd[1][1]) * root, (odd[1][1] - odd[1][0]) * root)
    odd[2] = minus_i(odd[2])
    odd[3] = ((odd[3][1] - odd[3][0]) * root, -(odd[3][0] + odd[3][1]) * root)
    return [add(even[k], odd[k]) for k in range(4)] + [sub(even[k], odd[k]) for k in range(4)]


def fold_kernel(
    facet_ref,
    corner_smem,
    corner_ref,
    member_ref,
    mixed_ref,
    columns_ref,
    edge_ref,
    out_ref,
    spread,
    cells,
    folded,
    lines,
):
    count = corner_ref.shape[0]
    anchor_x = facet_ref[0] % 4 * (GRID // FP // 4)
    anchor_y = facet_ref[0] // 4 % 4 * (GRID // FP // 4)
    folded[...] = jnp.zeros_like(folded)

    rows = 16

    def eight(step, carry):
        at = pl.ds(pl.multiple_of(step * rows, rows), rows)
        parts = []
        for source in range(GROUPS):
            pair = mixed_ref[source, at, :].astype(F32)
            parts.append((pair[:, :LANES], pair[:, LANES:]))
        for a_lo, value in enumerate(eight_point(parts)):
            spread[a_lo, at, :] = jnp.concatenate(value, axis=1).astype(BF16)
        return carry

    lax.fori_loop(0, count // rows, eight, 0)

    phase = (
        (corner_ref[:, 0:1] & (GRID - 1)) * anchor_x + (corner_ref[:, 1:2] & (GRID - 1)) * anchor_y
    ) & (GRID - 1)
    cos_corner, sin_corner = cos_sin(phase.astype(F32) * (1.0 / GRID))
    member = member_ref[...].astype(F32)
    cos_corner = cos_corner * member
    sin_corner = sin_corner * member
    lane = lax.broadcasted_iota(jnp.int32, (1, LANES), 1)
    for a_lo in range(GROUPS):
        offset = (8 * (lane // S) + a_lo) * anchor_x + lane % S * anchor_y
        cos_cell, sin_cell = cos_sin(offset.astype(F32) * (1.0 / GRID))
        cos_all = cos_corner * cos_cell - sin_corner * sin_cell
        sin_all = cos_corner * sin_cell + sin_corner * cos_cell
        value = dot(spread[a_lo], columns_ref[a_lo])
        real, imag = value[:, :LANES], value[:, LANES:]
        cells[pl.ds(a_lo * count, count), :] = real * cos_all - imag * sin_all
        cells[pl.ds((GROUPS + a_lo) * count, count), :] = real * sin_all + imag * cos_all

    lane8 = lax.broadcasted_iota(jnp.int32, (8, LANES), 1)

    def place(number, carry):
        first_u = corner_smem[number, 0] & (FP - 1)
        first_v = corner_smem[number, 1] & (FP - 1)
        tile = first_v // LANES
        within = first_v % LANES
        here = (lane8 >= within) & (lane8 < within + S)
        there = lane8 < within + S - LANES
        for part in range(2):
            block = cells[pl.ds(part * GROUPS * count + number, GROUPS, stride=count), :]
            for a_hi in range(RADIX):
                moved = pltpu.roll(block, (within - S * a_hi) & (LANES - 1), 1)
                at = pl.ds(first_u + 8 * a_hi, 8)
                folded[part, tile, at, :] += jnp.where(here, moved, 0.0)
                folded[part, tile + 1, at, :] += jnp.where(there, moved, 0.0)
        return carry

    lax.fori_loop(0, count, place, 0)

    for part in range(2):
        folded[part, :, 0:S, :] += folded[part, :, FP : FP + S, :]
        folded[part, 0] += folded[part, FP // LANES]
    tiles = FP // LANES
    for tile in range(tiles):
        real, imag = folded[0, tile, 0:FP, :], folded[1, tile, 0:FP, :]
        lines[0:FP, pl.ds(tile * LANES, LANES)] = real.astype(BF16)
        lines[FP : 2 * FP, pl.ds(tile * LANES, LANES)] = (-imag).astype(BF16)
        lines[0:FP, pl.ds(FP + tile * LANES, LANES)] = imag.astype(BF16)
        lines[FP : 2 * FP, pl.ds(FP + tile * LANES, LANES)] = real.astype(BF16)
    width = 256

    def transform(step, carry):
        at = pl.ds(pl.multiple_of(step * width, width), width)
        out_ref[:, at] = dot(edge_ref[...], lines[:, at]).astype(BF16)
        return carry

    lax.fori_loop(0, 2 * FP // width, transform, 0)


def fold_facet(facet, corners, members, mixed, edges):
    count = corners.shape[0]
    vmem = pl.BlockSpec(memory_space=pltpu.VMEM)
    smem = pl.BlockSpec(memory_space=pltpu.SMEM)
    return pl.pallas_call(
        fold_kernel,
        out_shape=jax.ShapeDtypeStruct((FP, 2 * FP), BF16),
        in_specs=[smem, smem, vmem, vmem, vmem, vmem, vmem],
        out_specs=vmem,
        scratch_shapes=[
            pltpu.VMEM((GROUPS, count, 2 * LANES), BF16),
            pltpu.VMEM((2 * GROUPS * count, LANES), F32),
            pltpu.VMEM((2, FP // LANES + 1, FP + S, LANES), F32),
            pltpu.VMEM((2 * FP, 2 * FP), BF16),
        ],
        name="fold_facet",
    )(facet.reshape(1), corners, corners, members, mixed, jnp.asarray(dft_columns_table()), edges)


def sum_kernel(scale, times, lines_ref, edge_ref, out_ref, pair, half, whole, send, recv, pair_send, pair_recv):
    time = lax.axis_index("tm")
    chips = times // 2
    core = lax.rem(time, 2)
    chip = time // 2
    other = time + 1 - 2 * core
    barrier = pltpu.get_barrier_semaphore()
    pl.semaphore_signal(barrier, inc=1, device_id={"tm": other}, device_id_type=MESH)
    for step in range(1, chips):
        target = lax.rem(chip + step, chips) * 2 + core
        pl.semaphore_signal(barrier, inc=1, device_id={"tm": target}, device_id_type=MESH)
    pl.semaphore_wait(barrier, chips)

    exchange = pltpu.make_async_remote_copy(
        src_ref=lines_ref.at[:, 1 - core],
        dst_ref=pair,
        send_sem=pair_send,
        recv_sem=pair_recv,
        device_id={"tm": other},
        device_id_type=MESH,
    )
    exchange.start()
    exchange.wait()
    half[...] = (lines_ref[:, core].astype(F32) + pair[...].astype(F32)).astype(BF16)
    copies = []
    for step in range(1, chips):
        target = lax.rem(chip + step, chips)
        copy = pltpu.make_async_remote_copy(
            src_ref=half.at[target],
            dst_ref=whole.at[chip],
            send_sem=send.at[step],
            recv_sem=recv.at[step],
            device_id={"tm": target * 2 + core},
            device_id_type=MESH,
        )
        copy.start()
        copies.append(copy)
    whole[chip] = half[chip]
    for copy in copies:
        copy.wait()
    total = whole[0].astype(F32)
    for source in range(1, chips):
        total = total + whole[source].astype(F32)
    total = total.astype(BF16)
    real, imag = total[:, :FP], total[:, FP:]
    cos_part, sin_part = edge_ref[:, :FP], edge_ref[:, FP:]
    out_ref[0] = (dot(real, cos_part) - dot(imag, sin_part)) * scale
    out_ref[1] = (dot(real, sin_part) + dot(imag, cos_part)) * scale


def sum_facet(lines, edges, scale, times):
    chips = times // 2
    rows = FP // times
    vmem = pl.BlockSpec(memory_space=pltpu.VMEM)
    return pl.pallas_call(
        functools.partial(sum_kernel, scale, times),
        out_shape=jax.ShapeDtypeStruct((2, rows, FP), F32),
        in_specs=[vmem] * 2,
        out_specs=vmem,
        scratch_shapes=[
            pltpu.VMEM((chips, rows, 2 * FP), BF16),
            pltpu.VMEM((chips, rows, 2 * FP), BF16),
            pltpu.VMEM((chips, rows, 2 * FP), BF16),
            pltpu.SemaphoreType.DMA((chips,)),
            pltpu.SemaphoreType.DMA((chips,)),
            pltpu.SemaphoreType.DMA,
            pltpu.SemaphoreType.DMA,
        ],
        compiler_params=pltpu.CompilerParams(collective_id=1, has_side_effects=True),
        name="sum_facet",
    )(lines.reshape(chips, 2, rows, 2 * FP), edges)


def per_device(
    visibilities, coordinates, station_screens, subgrid_stations, subgrid_corners, facet_member
):
    times = lax.axis_size("tm")
    facets = lax.axis_size("facet")
    facet = lax.axis_index("facet")
    screens = jnp.transpose(
        lax.dynamic_slice_in_dim(station_screens, facet * LANES, LANES, axis=3), (0, 2, 1, 3)
    )
    mixed = gather_rows(visibilities, coordinates, screens, subgrid_stations, facets, times)
    edges = jnp.asarray(facet_table())
    lines = fold_facet(facet, subgrid_corners, facet_member, mixed, edges)
    total_count = visibilities.shape[1] * facets * times
    scale = 1.0 / (S * math.sqrt(visibilities.shape[2] * total_count))
    own_rows = sum_facet(lines, edges, scale, times)
    return own_rows[:, None]


def solution(mesh):
    in_specs = (
        P(None, ("tm", "facet"), None),
        P(None, ("tm", "facet"), None),
        P(None, "tm", None, None),
        P("tm", None),
        P("tm", None),
        P("tm", "facet"),
    )
    out_specs = P(None, "facet", "tm", None)
    return jax.shard_map(
        per_device, mesh=mesh, in_specs=in_specs, out_specs=out_specs, check_vma=False
    )
```

profile of v0, /device:TPU:1, one launch (start us, length us, event | category | flops | bytes accessed | tf_op | source)
XLA Modules:
  0.0 75.8 jit_solution(12847334337383818914)
XLA Ops:
  0.0 0.0 copy-start
  0.0 0.9 %copy-done = bf16[2,16,2,1024]{3,2,1,0:T(2,128)(2,1)S(1)} copy-done((bf16[2,16,2,1024]{3,2,1,0:T(2,128)(2,1)S(1)}, bf16[2,16,2,1024]{3,2,1,0:T(2,128)(2,1)}, u32[]{:S(2)}) %copy-start) | copy-done | bytes 131096
  0.9 0.6 copy.19
  1.5 0.0 copy-start.1
  1.5 0.7 copy-done.1
  2.2 0.0 copy-start.2
  2.2 0.7 copy.12.station_ref
  2.9 0.0 copy-done.2
  2.9 0.0 copy-start.3
  2.9 0.7 copy.13.corner_smem.corner_ref
  3.7 0.0 copy-done.3
  3.7 0.7 copy.15.member_ref
  4.4 31.7 %subgrid_rows.1.mixed_ref = bf16[8,128,256]{2,1,0:T(8,128)(2,1)} custom-call(bf16[2,16,128]{2,1,0:T(8,128)(2,1)} %vis_ref.1, bf16[3,16,128]{2,1,0:T(8,128)(2,1)} %coord_ref.1, bf16[2,2,16,128]{3,2,1,0:T(8,128)(2,1)} %bitcast.10, s32[128,2]{1,0:T(8,128)} %copy.12.station_ref, f32[8,128]{1,0:T(8,128)} %constant.20.clone.taper_ref, ...), custom_call_target="tpu_custom_call" | custom-call | tf_op jit(solution)/shard_map/subgrid_rows/pallas_call | solution.py:223
  36.1 17.0 %fold_facet.1 = bf16[512,1024]{1,0:T(8,128)(2,1)} custom-call(s32[1]{0:T(128)} %bitcast.facet_ref, s32[128,2]{1,0:T(8,128)} %copy.13.corner_smem.corner_ref, s32[128,2]{1,0:T(8,128)} %copy.13.corner_smem.corner_ref, s32[128,1]{1,0:T(8,128)} %copy.15.member_ref, bf16[8,128,256]{2,1,0:T(8,128)(2,1)} %subgrid_rows.1.mixed_ref, ...), custom_call_target="tpu_custom_call" | custom-call | tf_op jit(solution)/shard_map/fold_facet/pallas_call | solution.py:373
  53.1 21.2 %sum_facet.1 = f32[2,16,512]{2,1,0:T(8,128)} custom-call(bf16[16,2,16,1024]{3,2,1,0:T(8,128)(2,1)} %bitcast.8, bf16[512,1024]{1,0:T(8,128)(2,1)} %constant.22.clone.edge_ref), custom_call_target="tpu_custom_call" | custom-call | tf_op jit(solution)/shard_map/sum_facet/pallas_call | solution.py:442
  74.3 1.5 %copy.21 = f32[2,1,16,512]{3,2,1,0:T(8,128)} copy(f32[2,1,16,512]{3,2,1,0:T(8,128)} %bitcast.9) | data formatting | bytes 131072
  (1 shorter events, 0.0 us)
Async XLA Ops:
  0.0 0.9 %copy-start = (bf16[2,16,2,1024]{3,2,1,0:T(2,128)(2,1)S(1)}, bf16[2,16,2,1024]{3,2,1,0:T(2,128)(2,1)}, u32[]{:S(2)}) copy-start(bf16[2,16,2,1024]{3,2,1,0:T(2,128)(2,1)} %param.12) | copy-start | bytes 393220
  1.5 0.7 copy-start.1
  2.2 0.7 copy-start.2
  2.9 0.7 copy-start.3
where the time goes:
time: 76.1 us; the launch traced here: 75.8 us
  Pallas kernels  69.9 us (92%)
  local copies, waits for them, and re-layouts  5.88 us (8%)
    pallas_call x1, Pallas kernels, gather_rows(): pl.pallas_call(functools.partial(rows_kernel, facets, times), out_shape=j...  31.7 us
    pallas_call x1, Pallas kernels, sum_facet(): pl.pallas_call(functools.partial(sum_kernel, scale, times), out_shape=jax...  21.2 us
    pallas_call x1, Pallas kernels, fold_facet(): pl.pallas_call(fold_kernel, out_shape=jax.ShapeDtypeStruct((FP, 2 * FP),...  17 us
    unnamed x13, local copies, waits for them, and re-layouts  5.86 us

commit v1 on v0

--- a/solution.py
+++ b/solution.py
@@ -9,6 +9,7 @@
 from jax.experimental.pallas import tpu as pltpu
 from jax.sharding import PartitionSpec as P
 
+UNROLL = 16
 GRID = 65536
 S = 32
 NT = 128
@@ -48,6 +49,14 @@
 def facet_table():
     angles = 2.0 * np.pi * (np.outer(np.arange(FP), np.arange(FP)) % FP) / FP
     return rounded(np.concatenate([np.cos(angles), np.sin(angles)], axis=1))
+
+
+def facet_rows_table():
+    tables = []
+    for residue in range(4):
+        angles = 2.0 * np.pi * (np.outer(np.arange(FP // 4), np.arange(residue, FP, 4)) % FP) / FP
+        tables.append(rounded(complex_block(np.exp(-1j * angles))))
+    return np.stack(tables)
 
 
 def taper_table():
@@ -175,14 +184,18 @@
     for copy in image_copies + screen_copies:
         copy.wait()
 
-    count = station_ref.shape[0]
+    count = station_ref.shape[1]
     stations = screens.shape[0] * screens.shape[2]
     screen_pair = jnp.concatenate(
         [screens[:, 0].reshape(stations, LANES), screens[:, 1].reshape(stations, LANES)], axis=1
     )
-    station = lax.broadcasted_iota(jnp.int32, (count, stations), 1)
-    first = dot((station == station_ref[:, 0:1]).astype(F32).astype(BF16), screen_pair)
-    second = dot((station == station_ref[:, 1:2]).astype(F32).astype(BF16), screen_pair)
+    wanted = jnp.concatenate(
+        [jnp.broadcast_to(station_ref[k : k + 1, :], (4, count)) for k in range(2)], axis=0
+    ).astype(F32)
+    wanted = wanted.T
+    station = lax.broadcasted_iota(jnp.int32, (count, stations), 1).astype(F32)
+    first = dot((station == wanted[:, 0:1]).astype(F32).astype(BF16), screen_pair)
+    second = dot((station == wanted[:, 4:5]).astype(F32).astype(BF16), screen_pair)
     first_real, first_imag = first[:, :LANES], first[:, LANES:]
     second_real, second_imag = second[:, :LANES], second[:, LANES:]
     taper = taper_ref[pl.ds(facet, 1), :]
@@ -218,7 +231,7 @@
 
 def gather_rows(visibilities, coordinates, screens, stations, facets, times):
     own = visibilities.shape[1]
-    count = stations.shape[0]
+    count = stations.shape[1]
     vmem = pl.BlockSpec(memory_space=pltpu.VMEM)
     return pl.pallas_call(
         functools.partial(rows_kernel, facets, times),
@@ -282,17 +295,18 @@
     member_ref,
     mixed_ref,
     columns_ref,
-    edge_ref,
     out_ref,
     spread,
     cells,
-    folded,
-    lines,
+    folded_real,
+    folded_imag,
 ):
-    count = corner_ref.shape[0]
+    count = corner_ref.shape[1]
     anchor_x = facet_ref[0] % 4 * (GRID // FP // 4)
     anchor_y = facet_ref[0] // 4 % 4 * (GRID // FP // 4)
-    folded[...] = jnp.zeros_like(folded)
+    folded = (folded_real, folded_imag)
+    for whole in folded:
+        whole[...] = jnp.zeros_like(whole)
 
     rows = 16
 
@@ -309,83 +323,101 @@
     lax.fori_loop(0, count // rows, eight, 0)
 
     phase = (
-        (corner_ref[:, 0:1] & (GRID - 1)) * anchor_x + (corner_ref[:, 1:2] & (GRID - 1)) * anchor_y
+        (corner_ref[0:1, :] & (GRID - 1)) * anchor_x + (corner_ref[1:2, :] & (GRID - 1)) * anchor_y
     ) & (GRID - 1)
     cos_corner, sin_corner = cos_sin(phase.astype(F32) * (1.0 / GRID))
     member = member_ref[...].astype(F32)
-    cos_corner = cos_corner * member
-    sin_corner = sin_corner * member
-    lane = lax.broadcasted_iota(jnp.int32, (1, LANES), 1)
+    pair = jnp.concatenate([cos_corner * member] * 4 + [sin_corner * member] * 4, axis=0).T
+    cos_corner, sin_corner = pair[:, 0:1], pair[:, 4:5]
+    lane = lax.broadcasted_iota(jnp.int32, (GROUPS, LANES), 1)
+    low = lax.broadcasted_iota(jnp.int32, (GROUPS, LANES), 0)
+    offset = (8 * (lane // S) + low) * anchor_x + lane % S * anchor_y
+    cos_cells, sin_cells = cos_sin(offset.astype(F32) * (1.0 / GRID))
     for a_lo in range(GROUPS):
-        offset = (8 * (lane // S) + a_lo) * anchor_x + lane % S * anchor_y
-        cos_cell, sin_cell = cos_sin(offset.astype(F32) * (1.0 / GRID))
+        cos_cell, sin_cell = cos_cells[a_lo : a_lo + 1], sin_cells[a_lo : a_lo + 1]
+        value = dot(spread[a_lo], columns_ref[a_lo])
+        real, imag = value[:, :LANES], value[:, LANES:]
         cos_all = cos_corner * cos_cell - sin_corner * sin_cell
         sin_all = cos_corner * sin_cell + sin_corner * cos_cell
-        value = dot(spread[a_lo], columns_ref[a_lo])
-        real, imag = value[:, :LANES], value[:, LANES:]
         cells[pl.ds(a_lo * count, count), :] = real * cos_all - imag * sin_all
         cells[pl.ds((GROUPS + a_lo) * count, count), :] = real * sin_all + imag * cos_all
 
     lane8 = lax.broadcasted_iota(jnp.int32, (8, LANES), 1)
 
-    def place(number, carry):
-        first_u = corner_smem[number, 0] & (FP - 1)
-        first_v = corner_smem[number, 1] & (FP - 1)
+    def prepare(number):
+        first_u = corner_smem[0, number] & (FP - 1)
+        first_v = corner_smem[1, number] & (FP - 1)
         tile = first_v // LANES
         within = first_v % LANES
         here = (lane8 >= within) & (lane8 < within + S)
         there = lane8 < within + S - LANES
+        pieces = []
         for part in range(2):
             block = cells[pl.ds(part * GROUPS * count + number, GROUPS, stride=count), :]
             for a_hi in range(RADIX):
                 moved = pltpu.roll(block, (within - S * a_hi) & (LANES - 1), 1)
                 at = pl.ds(first_u + 8 * a_hi, 8)
-                folded[part, tile, at, :] += jnp.where(here, moved, 0.0)
-                folded[part, tile + 1, at, :] += jnp.where(there, moved, 0.0)
+                pieces.append((folded[part], tile, at, jnp.where(here, moved, 0.0)))
+                pieces.append((folded[part], tile + 1, at, jnp.where(there, moved, 0.0)))
+        return pieces
+
+    def place(step, carry):
+        ready = [prepare(step * UNROLL + k) for k in range(UNROLL)]
+        for pieces in ready:
+            sums = [ref[tile, at, :] + value for ref, tile, at, value in pieces]
+            for (ref, tile, at, _), value in zip(pieces, sums):
+                ref[tile, at, :] = value
         return carry
 
-    lax.fori_loop(0, count, place, 0)
-
-    for part in range(2):
-        folded[part, :, 0:S, :] += folded[part, :, FP : FP + S, :]
-        folded[part, 0] += folded[part, FP // LANES]
+    lax.fori_loop(0, count // UNROLL, place, 0)
+
     tiles = FP // LANES
-    for tile in range(tiles):
-        real, imag = folded[0, tile, 0:FP, :], folded[1, tile, 0:FP, :]
-        lines[0:FP, pl.ds(tile * LANES, LANES)] = real.astype(BF16)
-        lines[FP : 2 * FP, pl.ds(tile * LANES, LANES)] = (-imag).astype(BF16)
-        lines[0:FP, pl.ds(FP + tile * LANES, LANES)] = imag.astype(BF16)
-        lines[FP : 2 * FP, pl.ds(FP + tile * LANES, LANES)] = real.astype(BF16)
-    width = 256
-
-    def transform(step, carry):
-        at = pl.ds(pl.multiple_of(step * width, width), width)
-        out_ref[:, at] = dot(edge_ref[...], lines[:, at]).astype(BF16)
-        return carry
-
-    lax.fori_loop(0, 2 * FP // width, transform, 0)
-
-
-def fold_facet(facet, corners, members, mixed, edges):
-    count = corners.shape[0]
+    for part, whole in enumerate(folded):
+        whole[:, 0:S, :] += whole[:, FP : FP + S, :]
+        whole[0, 0:FP, :] += whole[tiles, 0:FP, :]
+    for residue in range(4):
+        for part, whole in enumerate(folded):
+            for tile in range(tiles):
+                out_ref[
+                    pl.ds((2 * residue + part) * LANES, LANES), pl.ds(tile * LANES, LANES)
+                ] = whole[tile, pl.ds(residue, LANES, stride=4), :].astype(BF16)
+
+
+def fold_facet(facet, corners, members, mixed):
+    count = corners.shape[1]
     vmem = pl.BlockSpec(memory_space=pltpu.VMEM)
     smem = pl.BlockSpec(memory_space=pltpu.SMEM)
     return pl.pallas_call(
         fold_kernel,
-        out_shape=jax.ShapeDtypeStruct((FP, 2 * FP), BF16),
-        in_specs=[smem, smem, vmem, vmem, vmem, vmem, vmem],
+        out_shape=jax.ShapeDtypeStruct((2 * FP, FP), BF16),
+        in_specs=[smem, smem, vmem, vmem, vmem, vmem],
         out_specs=vmem,
         scratch_shapes=[
             pltpu.VMEM((GROUPS, count, 2 * LANES), BF16),
             pltpu.VMEM((2 * GROUPS * count, LANES), F32),
-            pltpu.VMEM((2, FP // LANES + 1, FP + S, LANES), F32),
-            pltpu.VMEM((2 * FP, 2 * FP), BF16),
+            pltpu.VMEM((FP // LANES + 1, FP + S, LANES), F32),
+            pltpu.VMEM((FP // LANES + 1, FP + S, LANES), F32),
         ],
         name="fold_facet",
-    )(facet.reshape(1), corners, corners, members, mixed, jnp.asarray(dft_columns_table()), edges)
-
-
-def sum_kernel(scale, times, lines_ref, edge_ref, out_ref, pair, half, whole, send, recv, pair_send, pair_recv):
+    )(facet.reshape(1), corners, corners, members, mixed, jnp.asarray(dft_columns_table()))
+
+
+def sum_kernel(
+    scale,
+    times,
+    folded_ref,
+    rows_ref,
+    edge_ref,
+    out_ref,
+    lines,
+    pair,
+    half,
+    whole,
+    send,
+    recv,
+    pair_send,
+    pair_recv,
+):
     time = lax.axis_index("tm")
     chips = times // 2
     core = lax.rem(time, 2)
@@ -396,66 +428,102 @@
     for step in range(1, chips):
         target = lax.rem(chip + step, chips) * 2 + core
         pl.semaphore_signal(barrier, inc=1, device_id={"tm": target}, device_id_type=MESH)
-    pl.semaphore_wait(barrier, chips)
-
-    exchange = pltpu.make_async_remote_copy(
-        src_ref=lines_ref.at[:, 1 - core],
-        dst_ref=pair,
-        send_sem=pair_send,
-        recv_sem=pair_recv,
-        device_id={"tm": other},
-        device_id_type=MESH,
-    )
-    exchange.start()
-    exchange.wait()
-    half[...] = (lines_ref[:, core].astype(F32) + pair[...].astype(F32)).astype(BF16)
+
+    parts, width = lines.shape[0], lines.shape[4] // 2
+    rows = lines.shape[3]
+    quarter = FP // 4
+    exchanges = []
+    for part in range(parts):
+        at = pl.ds(part * width, width)
+        terms = []
+        for residue in range(4):
+            value = dot(rows_ref[residue], folded_ref[pl.ds(residue * 2 * quarter, 2 * quarter), at])
+            terms.append((value[:quarter], value[quarter:]))
+        even_sum = [terms[0][k] + terms[2][k] for k in range(2)]
+        even_diff = [terms[0][k] - terms[2][k] for k in range(2)]
+        odd_sum = [terms[1][k] + terms[3][k] for k in range(2)]
+        odd_diff = [terms[3][1] - terms[1][1], terms[1][0] - terms[3][0]]
+        results = (
+            [even_sum[k] + odd_sum[k] for k in range(2)],
+            [even_diff[k] + odd_diff[k] for k in range(2)],
+            [even_sum[k] - odd_sum[k] for k in range(2)],
+            [even_diff[k] - odd_diff[k] for k in range(2)],
+        )
+        share = chips // 4
+        for block, result in enumerate(results):
+            for k in range(2):
+                lines[part, pl.ds(block * share, share), :, :, pl.ds(k * width, width)] = (
+                    result[k].astype(BF16).reshape(share, 2, rows, width)
+                )
+        if part == 0:
+            pl.semaphore_wait(barrier, chips)
+        exchange = pltpu.make_async_remote_copy(
+            src_ref=lines.at[part, :, 1 - core],
+            dst_ref=pair.at[part],
+            send_sem=pair_send.at[part],
+            recv_sem=pair_recv.at[part],
+            device_id={"tm": other},
+            device_id_type=MESH,
+        )
+        exchange.start()
+        exchanges.append(exchange)
+
     copies = []
-    for step in range(1, chips):
-        target = lax.rem(chip + step, chips)
-        copy = pltpu.make_async_remote_copy(
-            src_ref=half.at[target],
-            dst_ref=whole.at[chip],
-            send_sem=send.at[step],
-            recv_sem=recv.at[step],
-            device_id={"tm": target * 2 + core},
-            device_id_type=MESH,
-        )
-        copy.start()
-        copies.append(copy)
-    whole[chip] = half[chip]
+    for part in range(parts):
+        exchanges[part].wait()
+        half[part] = (lines[part, :, core].astype(F32) + pair[part].astype(F32)).astype(BF16)
+        for step in range(1, chips):
+            target = lax.rem(chip + step, chips)
+            copy = pltpu.make_async_remote_copy(
+                src_ref=half.at[part, target],
+                dst_ref=whole.at[part, chip],
+                send_sem=send.at[part, step],
+                recv_sem=recv.at[part, step],
+                device_id={"tm": target * 2 + core},
+                device_id_type=MESH,
+            )
+            copy.start()
+            copies.append(copy)
+        whole[part, chip] = half[part, chip]
     for copy in copies:
         copy.wait()
-    total = whole[0].astype(F32)
-    for source in range(1, chips):
-        total = total + whole[source].astype(F32)
-    total = total.astype(BF16)
-    real, imag = total[:, :FP], total[:, FP:]
+    totals = []
+    for part in range(parts):
+        total = whole[part, 0].astype(F32)
+        for source in range(1, chips):
+            total = total + whole[part, source].astype(F32)
+        totals.append(total.astype(BF16))
+    real = jnp.concatenate([total[:, :width] for total in totals], axis=1)
+    imag = jnp.concatenate([total[:, width:] for total in totals], axis=1)
     cos_part, sin_part = edge_ref[:, :FP], edge_ref[:, FP:]
     out_ref[0] = (dot(real, cos_part) - dot(imag, sin_part)) * scale
     out_ref[1] = (dot(real, sin_part) + dot(imag, cos_part)) * scale
 
 
-def sum_facet(lines, edges, scale, times):
+def sum_facet(folded, scale, times):
     chips = times // 2
     rows = FP // times
+    parts = 2
+    width = FP // parts
     vmem = pl.BlockSpec(memory_space=pltpu.VMEM)
     return pl.pallas_call(
         functools.partial(sum_kernel, scale, times),
         out_shape=jax.ShapeDtypeStruct((2, rows, FP), F32),
-        in_specs=[vmem] * 2,
+        in_specs=[vmem] * 3,
         out_specs=vmem,
         scratch_shapes=[
-            pltpu.VMEM((chips, rows, 2 * FP), BF16),
-            pltpu.VMEM((chips, rows, 2 * FP), BF16),
-            pltpu.VMEM((chips, rows, 2 * FP), BF16),
-            pltpu.SemaphoreType.DMA((chips,)),
-            pltpu.SemaphoreType.DMA((chips,)),
-            pltpu.SemaphoreType.DMA,
-            pltpu.SemaphoreType.DMA,
+            pltpu.VMEM((parts, chips, 2, rows, 2 * width), BF16),
+            pltpu.VMEM((parts, chips, rows, 2 * width), BF16),
+            pltpu.VMEM((parts, chips, rows, 2 * width), BF16),
+            pltpu.VMEM((parts, chips, rows, 2 * width), BF16),
+            pltpu.SemaphoreType.DMA((parts, chips)),
+            pltpu.SemaphoreType.DMA((parts, chips)),
+            pltpu.SemaphoreType.DMA((parts,)),
+            pltpu.SemaphoreType.DMA((parts,)),
         ],
         compiler_params=pltpu.CompilerParams(collective_id=1, has_side_effects=True),
         name="sum_facet",
-    )(lines.reshape(chips, 2, rows, 2 * FP), edges)
+    )(folded, jnp.asarray(facet_rows_table()), jnp.asarray(facet_table()))
 
 
 def per_device(
@@ -467,12 +535,13 @@
     screens = jnp.transpose(
         lax.dynamic_slice_in_dim(station_screens, facet * LANES, LANES, axis=3), (0, 2, 1, 3)
     )
-    mixed = gather_rows(visibilities, coordinates, screens, subgrid_stations, facets, times)
-    edges = jnp.asarray(facet_table())
-    lines = fold_facet(facet, subgrid_corners, facet_member, mixed, edges)
+    mixed = gather_rows(
+        visibilities, coordinates, screens, jnp.transpose(subgrid_stations), facets, times
+    )
+    folded = fold_facet(facet, jnp.transpose(subgrid_corners), jnp.transpose(facet_member), mixed)
     total_count = visibilities.shape[1] * facets * times
     scale = 1.0 / (S * math.sqrt(visibilities.shape[2] * total_count))
-    own_rows = sum_facet(lines, edges, scale, times)
+    own_rows = sum_facet(folded, scale, times)
     return own_rows[:, None]
 
 

time: 76.1 us -> 62.7 us (0.82)
  Pallas kernels: 69.9 us -> 59.5 us
  local copies, waits for them, and re-layouts: 5.88 us -> 3 us
    pallas_call x1, Pallas kernels: 17 us -> 5.59 us  [fold_facet(): pl.pallas_call(fold_kernel, out_shape=jax.ShapeDtypeStruct((2 * FP, FP),...]
    unnamed x13 -> x4, local copies, waits for them, and re-layouts: 5.86 us -> 2.99 us
    pallas_call x1, Pallas kernels: 21.2 us -> 22.1 us  [sum_facet(): pl.pallas_call(functools.partial(sum_kernel, scale, times), out_shape=jax...]
where the time goes in v1:
time: 62.7 us; the launch traced here: 62.5 us
  Pallas kernels  59.5 us (95%)
  local copies, waits for them, and re-layouts  3 us (5%)
    pallas_call x1, Pallas kernels, gather_rows(): pl.pallas_call(functools.partial(rows_kernel, facets, times), out_shape=j...  31.8 us
    pallas_call x1, Pallas kernels, sum_facet(): pl.pallas_call(functools.partial(sum_kernel, scale, times), out_shape=jax...  22.1 us
    pallas_call x1, Pallas kernels, fold_facet(): pl.pallas_call(fold_kernel, out_shape=jax.ShapeDtypeStruct((2 * FP, FP),...  5.59 us
    unnamed x4, local copies, waits for them, and re-layouts  2.99 us

profile of v1, /device:TPU:1, one launch (start us, length us, event | category | flops | bytes accessed | tf_op | source)
XLA Modules:
  0.0 62.5 jit_solution(7829483697003078828)
XLA Ops:
  0.0 0.0 copy-start
  0.0 0.9 %copy-done = bf16[2,16,2,1024]{3,2,1,0:T(2,128)(2,1)S(1)} copy-done((bf16[2,16,2,1024]{3,2,1,0:T(2,128)(2,1)S(1)}, bf16[2,16,2,1024]{3,2,1,0:T(2,128)(2,1)}, u32[]{:S(2)}) %copy-start) | copy-done | bytes 131096
  0.9 0.6 copy.16
  1.5 31.8 %subgrid_rows.1.mixed_ref = bf16[8,128,256]{2,1,0:T(8,128)(2,1)} custom-call(bf16[2,16,128]{2,1,0:T(8,128)(2,1)} %vis_ref.1, bf16[3,16,128]{2,1,0:T(8,128)(2,1)} %coord_ref.1, bf16[2,2,16,128]{3,2,1,0:T(8,128)(2,1)} %bitcast.11, s32[2,128]{1,0:T(2,128)} %bitcast.14, f32[8,128]{1,0:T(8,128)} %constant.22.clone.taper_ref, ...), custom_call_target="tpu_custom_call" | custom-call | tf_op jit(solution)/shard_map/subgrid_rows/pallas_call | solution.py:236
  33.3 5.6 %fold_facet.1.folded_ref = bf16[1024,512]{1,0:T(8,128)(2,1)} custom-call(s32[1]{0:T(128)} %bitcast.facet_ref, s32[2,128]{1,0:T(2,128)} %bitcast.12, s32[2,128]{1,0:T(2,128)} %bitcast.13, s32[1,128]{1,0:T(1,128)} %bitcast.15, bf16[8,128,256]{2,1,0:T(8,128)(2,1)} %subgrid_rows.1.mixed_ref, bf16[8,256,256]{2,1,0:T(8,128)(2,1)} %constant.24.clone.columns_ref), custom_call_target="tpu_custom_call" | custom-call | tf_op jit(solution)/shard_map/fold_facet/pallas_call | solution.py:390
  38.9 22.1 %sum_facet.1 = f32[2,16,512]{2,1,0:T(8,128)} custom-call(bf16[1024,512]{1,0:T(8,128)(2,1)} %fold_facet.1.folded_ref, bf16[4,256,256]{2,1,0:T(8,128)(2,1)} %constant.25.clone.rows_ref, bf16[512,1024]{1,0:T(8,128)(2,1)} %constant.26.clone.edge_ref), custom_call_target="tpu_custom_call" | custom-call | tf_op jit(solution)/shard_map/sum_facet/pallas_call | solution.py:509
  61.0 1.5 %copy.18 = f32[2,1,16,512]{3,2,1,0:T(8,128)} copy(f32[2,1,16,512]{3,2,1,0:T(8,128)} %bitcast.10) | data formatting | bytes 131072
  (1 shorter events, 0.0 us)
Async XLA Ops:
  0.0 0.9 %copy-start = (bf16[2,16,2,1024]{3,2,1,0:T(2,128)(2,1)S(1)}, bf16[2,16,2,1024]{3,2,1,0:T(2,128)(2,1)}, u32[]{:S(2)}) copy-start(bf16[2,16,2,1024]{3,2,1,0:T(2,128)(2,1)} %param.13) | copy-start | bytes 393220

commit v2 on v1

--- a/solution.py
+++ b/solution.py
@@ -112,6 +112,15 @@
         return carry
 
     lax.fori_loop(0, inputs_ref.shape[1], one, 0)
+
+
+def far_first(length):
+    return sorted(range(1, length), key=lambda step: -min(step, length - step))
+
+
+def facet_steps(facets):
+    steps = [(turn, step) for turn in range(facets // 4) for step in range(4) if turn or step]
+    return sorted(steps, key=lambda pair: -(2 * pair[0] + min(pair[1], 4 - pair[1])))
 
 
 def rows_kernel(
@@ -133,56 +142,96 @@
     image_recv,
     screen_send,
     screen_recv,
+    relay_send,
+    relay_recv,
     out_send,
     out_recv,
 ):
     facet = lax.axis_index("facet")
     time = lax.axis_index("tm")
+    length = times // 4
+    core = lax.rem(time, 2)
+    side = lax.rem(time // 2, 2)
+    place = time // 4
+
+    def at_time(at_place, at_side, at_core):
+        return at_place * 4 + at_side * 2 + at_core
+
+    chips = [(step, turn) for step in far_first(length) + [0] for turn in (1, 0)][:-1]
+    others = facet_steps(facets)
+
+    def facet_at(step):
+        return lax.rem(facet + step[0] * 4, facets) // 4 * 4 + lax.rem(facet + step[1], 4)
+
     barrier = pltpu.get_barrier_semaphore()
-    for step in range(1, facets):
-        pl.semaphore_signal(
-            barrier, inc=1, device_id={"facet": lax.rem(facet + step, facets)}, device_id_type=MESH
-        )
-    for step in range(1, times):
-        pl.semaphore_signal(barrier, inc=1, device_id={"tm": lax.rem(time + step, times)}, device_id_type=MESH)
+    for step, turn in chips:
+        target = at_time(lax.rem(place + step, length), lax.rem(side + turn, 2), core)
+        pl.semaphore_signal(barrier, inc=1, device_id={"tm": target}, device_id_type=MESH)
+    for step in others:
+        pl.semaphore_signal(barrier, inc=1, device_id={"facet": facet_at(step)}, device_id_type=MESH)
+    partner = at_time(place, side, 1 - core)
+    pl.semaphore_signal(barrier, inc=1, device_id={"tm": partner}, device_id_type=MESH)
 
     inputs[0:2] = vis_ref[...].astype(F32)
     inputs[2:5] = coord_ref[...].astype(F32)
-    pl.semaphore_wait(barrier, facets - 1 + times - 1)
-
+    own_images(inputs, image)
+    pl.semaphore_wait(barrier, len(chips) + len(others) + 1)
+
+    slab = time // (times // SLABS)
+    to_partner = pltpu.make_async_remote_copy(
+        src_ref=screen_ref.at[slab],
+        dst_ref=screens.at[time],
+        send_sem=relay_send.at[len(chips)],
+        recv_sem=relay_recv.at[len(chips)],
+        device_id={"tm": partner},
+        device_id_type=MESH,
+    )
+    to_partner.start()
     screen_copies = []
-    for step in range(1, times):
-        target = lax.rem(time + step, times)
+    for number, (step, turn) in enumerate(chips):
+        target = at_time(lax.rem(place + step, length), lax.rem(side + turn, 2), core)
         copy = pltpu.make_async_remote_copy(
             src_ref=screen_ref.at[target // (times // SLABS)],
             dst_ref=screens.at[time],
-            send_sem=screen_send.at[step],
-            recv_sem=screen_recv.at[step],
+            send_sem=screen_send.at[number],
+            recv_sem=screen_recv.at[number],
             device_id={"tm": target},
             device_id_type=MESH,
         )
         copy.start()
         screen_copies.append(copy)
-    screens[time] = screen_ref[time // (times // SLABS)]
-
-    own_images(inputs, image)
-
     image_copies = []
-    for step in range(1, facets):
-        target = lax.rem(facet + step, facets)
+    for number, step in enumerate(others):
+        target = facet_at(step)
         copy = pltpu.make_async_remote_copy(
             src_ref=image.at[target],
             dst_ref=images.at[facet],
-            send_sem=image_send.at[step],
-            recv_sem=image_recv.at[step],
+            send_sem=image_send.at[number],
+            recv_sem=image_recv.at[number],
             device_id={"facet": target},
             device_id_type=MESH,
         )
         copy.start()
         image_copies.append(copy)
+    screens[time] = screen_ref[slab]
     images[facet] = image[facet]
-    for copy in image_copies + screen_copies:
-        copy.wait()
+
+    relay_copies = [to_partner]
+    for number, (step, turn) in enumerate(chips):
+        screen_copies[number].wait_recv()
+        source = at_time(lax.rem(place + length - step, length), lax.rem(side + turn, 2), core)
+        copy = pltpu.make_async_remote_copy(
+            src_ref=screens.at[source],
+            dst_ref=screens.at[source],
+            send_sem=relay_send.at[number],
+            recv_sem=relay_recv.at[number],
+            device_id={"tm": partner},
+            device_id_type=MESH,
+        )
+        copy.start()
+        relay_copies.append(copy)
+    for copy in image_copies + relay_copies:
+        copy.wait_recv()
 
     count = station_ref.shape[1]
     stations = screens.shape[0] * screens.shape[2]
@@ -213,18 +262,20 @@
     mixed[...] = dot(weighted, table_ref[...]).astype(BF16)
 
     out_copies = []
-    for step in range(1, facets):
+    for number, step in enumerate(others):
         copy = pltpu.make_async_remote_copy(
             src_ref=mixed,
             dst_ref=out_ref.at[facet],
-            send_sem=out_send.at[step],
-            recv_sem=out_recv.at[step],
-            device_id={"facet": lax.rem(facet + step, facets)},
+            send_sem=out_send.at[number],
+            recv_sem=out_recv.at[number],
+            device_id={"facet": facet_at(step)},
             device_id_type=MESH,
         )
         copy.start()
         out_copies.append(copy)
     out_ref[facet] = mixed[...]
+    for copy in screen_copies + image_copies + relay_copies:
+        copy.wait_send()
     for copy in out_copies:
         copy.wait()
 
@@ -246,8 +297,10 @@
             pltpu.VMEM((count, 2 * LANES), BF16),
             pltpu.SemaphoreType.DMA((facets,)),
             pltpu.SemaphoreType.DMA((facets,)),
-            pltpu.SemaphoreType.DMA((times,)),
-            pltpu.SemaphoreType.DMA((times,)),
+            pltpu.SemaphoreType.DMA((times // 2,)),
+            pltpu.SemaphoreType.DMA((times // 2,)),
+            pltpu.SemaphoreType.DMA((times // 2,)),
+            pltpu.SemaphoreType.DMA((times // 2,)),
             pltpu.SemaphoreType.DMA((facets,)),
             pltpu.SemaphoreType.DMA((facets,)),
         ],
@@ -411,33 +464,45 @@
     out_ref,
     lines,
     pair,
-    half,
-    whole,
-    send,
-    recv,
+    beside_out,
+    beside,
+    ring_out,
+    ring,
     pair_send,
     pair_recv,
+    beside_send,
+    beside_recv,
+    ring_send,
+    ring_recv,
 ):
     time = lax.axis_index("tm")
-    chips = times // 2
+    length = times // 4
     core = lax.rem(time, 2)
-    chip = time // 2
-    other = time + 1 - 2 * core
+    side = lax.rem(time // 2, 2)
+    place = time // 4
+    order = far_first(length) + [0]
+
+    def device(at_place, at_side, at_core):
+        return {"tm": at_place * 4 + at_side * 2 + at_core}
+
     barrier = pltpu.get_barrier_semaphore()
-    pl.semaphore_signal(barrier, inc=1, device_id={"tm": other}, device_id_type=MESH)
-    for step in range(1, chips):
-        target = lax.rem(chip + step, chips) * 2 + core
-        pl.semaphore_signal(barrier, inc=1, device_id={"tm": target}, device_id_type=MESH)
-
-    parts, width = lines.shape[0], lines.shape[4] // 2
+    for step in far_first(length):
+        pl.semaphore_signal(
+            barrier, inc=1, device_id=device(lax.rem(place + step, length), side, core), device_id_type=MESH
+        )
+    pl.semaphore_signal(barrier, inc=1, device_id=device(place, 1 - side, core), device_id_type=MESH)
+    pl.semaphore_signal(barrier, inc=1, device_id=device(place, side, 1 - core), device_id_type=MESH)
+
     rows = lines.shape[3]
     quarter = FP // 4
-    exchanges = []
-    for part in range(parts):
-        at = pl.ds(part * width, width)
+    width = 256
+    share = length // 4
+    for start in range(0, FP, width):
         terms = []
         for residue in range(4):
-            value = dot(rows_ref[residue], folded_ref[pl.ds(residue * 2 * quarter, 2 * quarter), at])
+            value = dot(
+                rows_ref[residue], folded_ref[pl.ds(residue * 2 * quarter, 2 * quarter), pl.ds(start, width)]
+            )
             terms.append((value[:quarter], value[quarter:]))
         even_sum = [terms[0][k] + terms[2][k] for k in range(2)]
         even_diff = [terms[0][k] - terms[2][k] for k in range(2)]
@@ -449,78 +514,97 @@
             [even_sum[k] - odd_sum[k] for k in range(2)],
             [even_diff[k] - odd_diff[k] for k in range(2)],
         )
-        share = chips // 4
         for block, result in enumerate(results):
             for k in range(2):
-                lines[part, pl.ds(block * share, share), :, :, pl.ds(k * width, width)] = (
-                    result[k].astype(BF16).reshape(share, 2, rows, width)
+                lines[pl.ds(block * share, share), :, :, :, pl.ds(k * FP + start, width)] = (
+                    result[k].astype(BF16).reshape(share, 2, 2, rows, width)
                 )
-        if part == 0:
-            pl.semaphore_wait(barrier, chips)
-        exchange = pltpu.make_async_remote_copy(
-            src_ref=lines.at[part, :, 1 - core],
-            dst_ref=pair.at[part],
-            send_sem=pair_send.at[part],
-            recv_sem=pair_recv.at[part],
-            device_id={"tm": other},
+    pl.semaphore_wait(barrier, length + 1)
+
+    copies = []
+    for step in order:
+        target = lax.rem(place + step, length)
+        copy = pltpu.make_async_remote_copy(
+            src_ref=lines.at[target, :, 1 - core],
+            dst_ref=pair.at[target],
+            send_sem=pair_send.at[step],
+            recv_sem=pair_recv.at[step],
+            device_id=device(place, side, 1 - core),
             device_id_type=MESH,
         )
-        exchange.start()
-        exchanges.append(exchange)
-
-    copies = []
-    for part in range(parts):
-        exchanges[part].wait()
-        half[part] = (lines[part, :, core].astype(F32) + pair[part].astype(F32)).astype(BF16)
-        for step in range(1, chips):
-            target = lax.rem(chip + step, chips)
-            copy = pltpu.make_async_remote_copy(
-                src_ref=half.at[part, target],
-                dst_ref=whole.at[part, chip],
-                send_sem=send.at[part, step],
-                recv_sem=recv.at[part, step],
-                device_id={"tm": target * 2 + core},
-                device_id_type=MESH,
-            )
-            copy.start()
-            copies.append(copy)
-        whole[part, chip] = half[part, chip]
-    for copy in copies:
-        copy.wait()
-    totals = []
-    for part in range(parts):
-        total = whole[part, 0].astype(F32)
-        for source in range(1, chips):
-            total = total + whole[part, source].astype(F32)
-        totals.append(total.astype(BF16))
-    real = jnp.concatenate([total[:, :width] for total in totals], axis=1)
-    imag = jnp.concatenate([total[:, width:] for total in totals], axis=1)
+        copy.start()
+        copies.append(copy)
+    beside_copies = []
+    for step, copy in zip(order, copies):
+        target = lax.rem(place + step, length)
+        copy.wait_recv()
+        beside_out[target] = (
+            lines[target, 1 - side, core].astype(F32) + pair[target, 1 - side].astype(F32)
+        ).astype(BF16)
+        onward = pltpu.make_async_remote_copy(
+            src_ref=beside_out.at[target],
+            dst_ref=beside.at[target],
+            send_sem=beside_send.at[step],
+            recv_sem=beside_recv.at[step],
+            device_id=device(place, 1 - side, core),
+            device_id_type=MESH,
+        )
+        onward.start()
+        beside_copies.append(onward)
+    ring_copies = []
+    for step, copy in zip(order, beside_copies):
+        target = lax.rem(place + step, length)
+        copy.wait_recv()
+        value = (
+            lines[target, side, core].astype(F32)
+            + pair[target, side].astype(F32)
+            + beside[target].astype(F32)
+        )
+        if step == 0:
+            total = value
+            continue
+        ring_out[target] = value.astype(BF16)
+        onward = pltpu.make_async_remote_copy(
+            src_ref=ring_out.at[target],
+            dst_ref=ring.at[place],
+            send_sem=ring_send.at[step],
+            recv_sem=ring_recv.at[step],
+            device_id=device(target, side, core),
+            device_id_type=MESH,
+        )
+        onward.start()
+        ring_copies.append(onward)
+    for step, copy in zip(order, ring_copies):
+        copy.wait_recv()
+        total = total + ring[lax.rem(place + length - step, length)].astype(F32)
+    total = total.astype(BF16)
+    real, imag = total[:, :FP], total[:, FP:]
     cos_part, sin_part = edge_ref[:, :FP], edge_ref[:, FP:]
     out_ref[0] = (dot(real, cos_part) - dot(imag, sin_part)) * scale
     out_ref[1] = (dot(real, sin_part) + dot(imag, cos_part)) * scale
+    for copy in copies + beside_copies + ring_copies:
+        copy.wait_send()
 
 
 def sum_facet(folded, scale, times):
-    chips = times // 2
+    length = times // 4
     rows = FP // times
-    parts = 2
-    width = FP // parts
     vmem = pl.BlockSpec(memory_space=pltpu.VMEM)
+    block = pltpu.VMEM((length, rows, 2 * FP), BF16)
     return pl.pallas_call(
         functools.partial(sum_kernel, scale, times),
         out_shape=jax.ShapeDtypeStruct((2, rows, FP), F32),
         in_specs=[vmem] * 3,
         out_specs=vmem,
         scratch_shapes=[
-            pltpu.VMEM((parts, chips, 2, rows, 2 * width), BF16),
-            pltpu.VMEM((parts, chips, rows, 2 * width), BF16),
-            pltpu.VMEM((parts, chips, rows, 2 * width), BF16),
-            pltpu.VMEM((parts, chips, rows, 2 * width), BF16),
-            pltpu.SemaphoreType.DMA((parts, chips)),
-            pltpu.SemaphoreType.DMA((parts, chips)),
-            pltpu.SemaphoreType.DMA((parts,)),
-            pltpu.SemaphoreType.DMA((parts,)),
-        ],
+            pltpu.VMEM((length, 2, 2, rows, 2 * FP), BF16),
+            pltpu.VMEM((length, 2, rows, 2 * FP), BF16),
+            block,
+            block,
+            block,
+            block,
+        ]
+        + [pltpu.SemaphoreType.DMA((length,))] * 6,
         compiler_params=pltpu.CompilerParams(collective_id=1, has_side_effects=True),
         name="sum_facet",
     )(folded, jnp.asarray(facet_rows_table()), jnp.asarray(facet_table()))

time: 62.7 us -> 54.7 us (0.87)
  Pallas kernels: 59.5 us -> 51.4 us
    pallas_call x1, Pallas kernels: 22.1 us -> 17.6 us  [sum_facet(): pl.pallas_call(functools.partial(sum_kernel, scale, times), out_shape=jax...]
    pallas_call x1, Pallas kernels: 31.8 us -> 28.2 us  [gather_rows(): pl.pallas_call(functools.partial(rows_kernel, facets, times), out_shape=j...]
where the time goes in v2:
time: 54.7 us; the launch traced here: 54.4 us
  Pallas kernels  51.4 us (94%)
  local copies, waits for them, and re-layouts  3 us (5%)
    pallas_call x1, Pallas kernels, gather_rows(): pl.pallas_call(functools.partial(rows_kernel, facets, times), out_shape=j...  28.2 us
    pallas_call x1, Pallas kernels, sum_facet(): pl.pallas_call(functools.partial(sum_kernel, scale, times), out_shape=jax...  17.6 us
    pallas_call x1, Pallas kernels, fold_facet(): pl.pallas_call(fold_kernel, out_shape=jax.ShapeDtypeStruct((2 * FP, FP),...  5.6 us
    unnamed x4, local copies, waits for them, and re-layouts  2.99 us

profile of v2, /device:TPU:1, one launch (start us, length us, event | category | flops | bytes accessed | tf_op | source)
XLA Modules:
  0.0 54.4 jit_solution(18303773648542286864)
XLA Ops:
  0.0 0.0 copy-start
  0.0 0.9 %copy-done = bf16[2,16,2,1024]{3,2,1,0:T(2,128)(2,1)S(1)} copy-done((bf16[2,16,2,1024]{3,2,1,0:T(2,128)(2,1)S(1)}, bf16[2,16,2,1024]{3,2,1,0:T(2,128)(2,1)}, u32[]{:S(2)}) %copy-start) | copy-done | bytes 131096
  0.9 0.6 %copy.16 = bf16[2,16,2,128]{3,1,2,0:T(8,128)(2,1)} copy(bf16[2,16,2,128]{3,2,1,0:T(2,128)(2,1)S(1)} %constant_dynamic-slice_fusion) | data formatting | bytes 32768
  1.5 28.2 %subgrid_rows.1.mixed_ref = bf16[8,128,256]{2,1,0:T(8,128)(2,1)} custom-call(bf16[2,16,128]{2,1,0:T(8,128)(2,1)} %vis_ref.1, bf16[3,16,128]{2,1,0:T(8,128)(2,1)} %coord_ref.1, bf16[2,2,16,128]{3,2,1,0:T(8,128)(2,1)} %bitcast.11, s32[2,128]{1,0:T(2,128)} %bitcast.14, f32[8,128]{1,0:T(8,128)} %constant.22.clone.taper_ref, ...), custom_call_target="tpu_custom_call" | custom-call | tf_op jit(solution)/shard_map/subgrid_rows/pallas_call | solution.py:287
  29.8 5.6 %fold_facet.1.folded_ref = bf16[1024,512]{1,0:T(8,128)(2,1)} custom-call(s32[1]{0:T(128)} %bitcast.facet_ref, s32[2,128]{1,0:T(2,128)} %bitcast.12, s32[2,128]{1,0:T(2,128)} %bitcast.13, s32[1,128]{1,0:T(1,128)} %bitcast.15, bf16[8,128,256]{2,1,0:T(8,128)(2,1)} %subgrid_rows.1.mixed_ref, bf16[8,256,256]{2,1,0:T(8,128)(2,1)} %constant.24.clone.columns_ref), custom_call_target="tpu_custom_call" | custom-call | tf_op jit(solution)/shard_map/fold_facet/pallas_call | solution.py:443
  35.4 17.6 %sum_facet.1 = f32[2,16,512]{2,1,0:T(8,128)} custom-call(bf16[1024,512]{1,0:T(8,128)(2,1)} %fold_facet.1.folded_ref, bf16[4,256,256]{2,1,0:T(8,128)(2,1)} %constant.25.clone.rows_ref, bf16[512,1024]{1,0:T(8,128)(2,1)} %constant.26.clone.edge_ref), custom_call_target="tpu_custom_call" | custom-call | tf_op jit(solution)/shard_map/sum_facet/pallas_call | solution.py:594
  53.0 1.5 %copy.18 = f32[2,1,16,512]{3,2,1,0:T(8,128)} copy(f32[2,1,16,512]{3,2,1,0:T(8,128)} %bitcast.10) | data formatting | bytes 131072
  (1 shorter events, 0.0 us)
Async XLA Ops:
  0.0 0.9 %copy-start = (bf16[2,16,2,1024]{3,2,1,0:T(2,128)(2,1)S(1)}, bf16[2,16,2,1024]{3,2,1,0:T(2,128)(2,1)}, u32[]{:S(2)}) copy-start(bf16[2,16,2,1024]{3,2,1,0:T(2,128)(2,1)} %param.13) | copy-start | bytes 393220

commit v3 on v2

--- a/solution.py
+++ b/solution.py
@@ -10,6 +10,7 @@
 from jax.sharding import PartitionSpec as P
 
 UNROLL = 16
+VMEM_LIMIT = 24 * 2**20
 GRID = 65536
 S = 32
 NT = 128
@@ -32,9 +33,15 @@
 
 
 def dft_rows_table():
-    offsets = np.arange(S) - S // 2
-    table = np.exp(-2j * np.pi * (np.outer(offsets, offsets) % S) / S) / math.sqrt(S)
-    return rounded(complex_block(np.kron(np.eye(RADIX), table.T)))
+    source = lax.broadcasted_iota(jnp.int32, (LANES, LANES), 0)
+    target = lax.broadcasted_iota(jnp.int32, (LANES, LANES), 1)
+    phase = (source % S - S // 2) * (target % S - S // 2) & (S - 1)
+    cos_part, sin_part = cos_sin(phase.astype(F32) * (1.0 / S))
+    same = jnp.where(source // S == target // S, 1.0 / math.sqrt(S), 0.0)
+    real, imag = cos_part * same, sin_part * -same
+    return jnp.concatenate(
+        [jnp.concatenate([real, imag], axis=1), jnp.concatenate([-imag, real], axis=1)], axis=0
+    ).astype(BF16)
 
 
 def dft_columns_table():
@@ -57,11 +64,6 @@
         angles = 2.0 * np.pi * (np.outer(np.arange(FP // 4), np.arange(residue, FP, 4)) % FP) / FP
         tables.append(rounded(complex_block(np.exp(-1j * angles))))
     return np.stack(tables)
-
-
-def taper_table():
-    centre = np.sin(np.pi * (np.arange(S) + 0.5) / S)
-    return np.outer(centre, centre).reshape(GROUPS, LANES).astype(np.float32)
 
 
 def cos_sin(turns):
@@ -130,14 +132,13 @@
     coord_ref,
     screen_ref,
     station_ref,
-    taper_ref,
-    table_ref,
     out_ref,
     inputs,
     image,
     images,
     screens,
     mixed,
+    table,
     image_send,
     image_recv,
     screen_send,
@@ -216,6 +217,7 @@
     screens[time] = screen_ref[slab]
     images[facet] = image[facet]
 
+    table[...] = dft_rows_table()
     relay_copies = [to_partner]
     for number, (step, turn) in enumerate(chips):
         screen_copies[number].wait_recv()
@@ -247,7 +249,10 @@
     second = dot((station == wanted[:, 4:5]).astype(F32).astype(BF16), screen_pair)
     first_real, first_imag = first[:, :LANES], first[:, LANES:]
     second_real, second_imag = second[:, :LANES], second[:, LANES:]
-    taper = taper_ref[pl.ds(facet, 1), :]
+    lane = lax.broadcasted_iota(jnp.int32, (GROUPS, LANES), 1)
+    _, taper_row = cos_sin((RADIX * facet + lane // S).astype(F32) * (0.5 / S) + 0.25 / S)
+    _, taper_column = cos_sin((lane % S).astype(F32) * (0.5 / S) + 0.25 / S)
+    taper = (taper_row * taper_column)[0:1]
     weight_real = taper * (first_real * second_real + first_imag * second_imag)
     weight_imag = taper * (first_real * second_imag - first_imag * second_real)
     image_real = images[:, 0].reshape(count, LANES)
@@ -259,7 +264,7 @@
         ],
         axis=1,
     ).astype(BF16)
-    mixed[...] = dot(weighted, table_ref[...]).astype(BF16)
+    mixed[...] = dot(weighted, table[...]).astype(BF16)
 
     out_copies = []
     for number, step in enumerate(others):
@@ -287,7 +292,7 @@
     return pl.pallas_call(
         functools.partial(rows_kernel, facets, times),
         out_shape=jax.ShapeDtypeStruct((facets, count, 2 * LANES), BF16),
-        in_specs=[vmem] * 6,
+        in_specs=[vmem] * 4,
         out_specs=vmem,
         scratch_shapes=[
             pltpu.VMEM((5, own, NT), F32),
@@ -295,6 +300,7 @@
             pltpu.VMEM((GROUPS, 2, own, LANES), F32),
             pltpu.VMEM((times,) + screens.shape[1:], BF16),
             pltpu.VMEM((count, 2 * LANES), BF16),
+            pltpu.VMEM((2 * LANES, 2 * LANES), BF16),
             pltpu.SemaphoreType.DMA((facets,)),
             pltpu.SemaphoreType.DMA((facets,)),
             pltpu.SemaphoreType.DMA((times // 2,)),
@@ -304,15 +310,16 @@
             pltpu.SemaphoreType.DMA((facets,)),
             pltpu.SemaphoreType.DMA((facets,)),
         ],
-        compiler_params=pltpu.CompilerParams(collective_id=0, has_side_effects=True),
+        compiler_params=pltpu.CompilerParams(
+            collective_id=0, has_side_effects=True, vmem_limit_bytes=VMEM_LIMIT
+        ),
+        cost_estimate=pl.CostEstimate(flops=2 * 10**9, bytes_accessed=10**7, transcendentals=0),
         name="subgrid_rows",
     )(
         visibilities,
         coordinates,
         screens,
         stations,
-        jnp.asarray(taper_table()),
-        jnp.asarray(dft_rows_table()),
     )
 
 
@@ -451,6 +458,7 @@
             pltpu.VMEM((FP // LANES + 1, FP + S, LANES), F32),
             pltpu.VMEM((FP // LANES + 1, FP + S, LANES), F32),
         ],
+        compiler_params=pltpu.CompilerParams(vmem_limit_bytes=VMEM_LIMIT),
         name="fold_facet",
     )(facet.reshape(1), corners, corners, members, mixed, jnp.asarray(dft_columns_table()))
 
@@ -605,7 +613,9 @@
             block,
         ]
         + [pltpu.SemaphoreType.DMA((length,))] * 6,
-        compiler_params=pltpu.CompilerParams(collective_id=1, has_side_effects=True),
+        compiler_params=pltpu.CompilerParams(
+            collective_id=1, has_side_effects=True, vmem_limit_bytes=VMEM_LIMIT
+        ),
         name="sum_facet",
     )(folded, jnp.asarray(facet_rows_table()), jnp.asarray(facet_table()))
 

time: 54.7 us -> 48.4 us (0.88)
  Pallas kernels: 51.4 us -> 45.8 us
  local copies, waits for them, and re-layouts: 3 us -> 2.27 us
    pallas_call x1, Pallas kernels: 17.6 us -> 15.4 us  [sum_facet(): pl.pallas_call(functools.partial(sum_kernel, scale, times), out_shape=jax...]
    pallas_call x1, Pallas kernels: 5.6 us -> 3.73 us  [fold_facet(): pl.pallas_call(fold_kernel, out_shape=jax.ShapeDtypeStruct((2 * FP, FP),...]
    pallas_call x1, Pallas kernels: 28.2 us -> 26.6 us  [gather_rows(): pl.pallas_call(functools.partial(rows_kernel, facets, times), out_shape=j...]
    unnamed x4 -> x20, local copies, waits for them, and re-layouts: 2.99 us -> 2.25 us
where the time goes in v3:
time: 48.4 us; the launch traced here: 48.2 us
  Pallas kernels  45.8 us (95%)
  local copies, waits for them, and re-layouts  2.27 us (5%)
    pallas_call x1, Pallas kernels, gather_rows(): pl.pallas_call(functools.partial(rows_kernel, facets, times), out_shape=j...  26.6 us
    pallas_call x1, Pallas kernels, sum_facet(): pl.pallas_call(functools.partial(sum_kernel, scale, times), out_shape=jax...  15.4 us
    pallas_call x1, Pallas kernels, fold_facet(): pl.pallas_call(fold_kernel, out_shape=jax.ShapeDtypeStruct((2 * FP, FP),...  3.73 us
    unnamed x20, local copies, waits for them, and re-layouts  2.25 us

profile of v3, /device:TPU:1, one launch (start us, length us, event | category | flops | bytes accessed | tf_op | source)
XLA Modules:
  0.0 48.2 jit_solution(14398152436631534371)
XLA Ops:
  0.0 0.0 copy-start
  0.0 0.9 %copy-done = bf16[2,16,2,1024]{3,2,1,0:T(2,128)(2,1)S(1)} copy-done((bf16[2,16,2,1024]{3,2,1,0:T(2,128)(2,1)S(1)}, bf16[2,16,2,1024]{3,2,1,0:T(2,128)(2,1)}, u32[]{:S(2)}) %copy-start) | copy-done | bytes 131096
  0.9 0.0 copy-start.6
  0.9 0.0 copy-start.7
  1.0 0.0 copy-start.8
  1.0 0.7 %copy-done.6 = bf16[3,16,128]{2,1,0:T(8,128)(2,1)S(1)} copy-done((bf16[3,16,128]{2,1,0:T(8,128)(2,1)S(1)}, bf16[3,16,128]{2,1,0:T(8,128)(2,1)}, u32[]{:S(2)}) %copy-start.6) | copy-done | bytes 12312
  1.6 0.0 copy-done.7
  1.6 0.0 copy-done.8
  1.6 0.0 copy-start.1
  1.6 0.0 copy-start.4
  1.6 0.0 copy-start.5
  1.7 26.6 %subgrid_rows.1.mixed_ref = bf16[8,128,256]{2,1,0:T(8,128)(2,1)S(1)} custom-call(bf16[2,16,128]{2,1,0:T(8,128)(2,1)S(1)} %copy-done.7, bf16[3,16,128]{2,1,0:T(8,128)(2,1)S(1)} %copy-done.6, bf16[2,2,16,128]{3,2,1,0:T(8,128)(2,1)S(1)} %bitcast.11, s32[2,128]{1,0:T(2,128)S(1)} %bitcast.15), custom_call_target="tpu_custom_call" | custom-call | flops 2000000000 | bytes 10000000 | tf_op jit(solution)/shard_map/subgrid_rows/pallas_call | solution.py:292
  28.3 0.0 copy-done.1
  28.3 0.0 copy-done.4
  28.3 0.0 copy-done.5
  28.3 0.0 copy-start.2
  28.4 0.0 copy-start.3
  28.4 3.7 %fold_facet.1.folded_ref = bf16[1024,512]{1,0:T(8,128)(2,1)S(1)} custom-call(s32[1]{0:T(128)} %bitcast.facet_ref, s32[2,128]{1,0:T(2,128)S(1)} %bitcast.12, s32[2,128]{1,0:T(2,128)S(1)} %bitcast.13, s32[1,128]{1,0:T(1,128)S(1)} %bitcast.14, bf16[8,128,256]{2,1,0:T(8,128)(2,1)S(1)} %subgrid_rows.1.mixed_ref, bf16[8,256,256]{2,1,0:T(8,128)(2,1)S(1)} %copy-done.1), custom_call_target="tpu_custom_call" | custom-call | tf_op jit(solution)/shard_map/fold_facet/pallas_call | solution.py:450
  32.1 0.0 copy-done.2
  32.1 0.0 copy-done.3
  32.1 15.4 %sum_facet.1 = f32[2,16,512]{2,1,0:T(8,128)S(1)} custom-call(bf16[1024,512]{1,0:T(8,128)(2,1)S(1)} %fold_facet.1.folded_ref, bf16[4,256,256]{2,1,0:T(8,128)(2,1)S(1)} %copy-done.3, bf16[512,1024]{1,0:T(8,128)(2,1)S(1)} %copy-done.2), custom_call_target="tpu_custom_call" | custom-call | tf_op jit(solution)/shard_map/sum_facet/pallas_call | solution.py:602
  47.6 0.6 %copy.16 = f32[2,1,16,512]{3,2,1,0:T(8,128)} copy(f32[2,1,16,512]{3,2,1,0:T(8,128)S(1)} %bitcast.10) | data formatting | bytes 131072
  (2 shorter events, 0.0 us)
Async XLA Ops:
  0.0 0.9 %copy-start = (bf16[2,16,2,1024]{3,2,1,0:T(2,128)(2,1)S(1)}, bf16[2,16,2,1024]{3,2,1,0:T(2,128)(2,1)}, u32[]{:S(2)}) copy-start(bf16[2,16,2,1024]{3,2,1,0:T(2,128)(2,1)} %param.11) | copy-start | bytes 393220
  0.9 0.7 %copy-start.6 = (bf16[3,16,128]{2,1,0:T(8,128)(2,1)S(1)}, bf16[3,16,128]{2,1,0:T(8,128)(2,1)}, u32[]{:S(2)}) copy-start(bf16[3,16,128]{2,1,0:T(8,128)(2,1)} %coord_ref.1) | copy-start | bytes 36868
  0.9 0.7 %copy-start.7 = (bf16[2,16,128]{2,1,0:T(8,128)(2,1)S(1)}, bf16[2,16,128]{2,1,0:T(8,128)(2,1)}, u32[]{:S(2)}) copy-start(bf16[2,16,128]{2,1,0:T(8,128)(2,1)} %vis_ref.1) | copy-start | bytes 24580
  1.0 0.7 %copy-start.8 = (s32[128,2]{0,1:T(2,128)S(1)}, s32[128,2]{0,1:T(2,128)}, u32[]{:S(2)}) copy-start(s32[128,2]{0,1:T(2,128)} %param.12) | copy-start | bytes 3076
  1.6 26.7 %copy-start.1 = (bf16[8,256,256]{2,1,0:T(8,128)(2,1)S(1)}, bf16[8,256,256]{2,1,0:T(8,128)(2,1)}, u32[]{:S(2)}) copy-start(bf16[8,256,256]{2,1,0:T(8,128)(2,1)} %constant.18.clone.columns_ref) | copy-start | bytes 3145732
  1.6 26.7 %copy-start.4 = (s32[128,2]{0,1:T(2,128)S(1)}, s32[128,2]{0,1:T(2,128)}, u32[]{:S(2)}) copy-start(s32[128,2]{0,1:T(2,128)} %param.13) | copy-start | bytes 3076
  1.6 26.7 %copy-start.5 = (s32[128,1]{0,1:T(1,128)S(1)}, s32[128,1]{0,1:T(1,128)}, u32[]{:S(2)}) copy-start(s32[128,1]{0,1:T(1,128)} %param.14) | copy-start | bytes 1540
  28.3 3.8 %copy-start.2 = (bf16[512,1024]{1,0:T(8,128)(2,1)S(1)}, bf16[512,1024]{1,0:T(8,128)(2,1)}, u32[]{:S(2)}) copy-start(bf16[512,1024]{1,0:T(8,128)(2,1)} %constant.20.clone.edge_ref) | copy-start | bytes 3145732
  28.4 3.8 %copy-start.3 = (bf16[4,256,256]{2,1,0:T(8,128)(2,1)S(1)}, bf16[4,256,256]{2,1,0:T(8,128)(2,1)}, u32[]{:S(2)}) copy-start(bf16[4,256,256]{2,1,0:T(8,128)(2,1)} %constant.19.clone.rows_ref) | copy-start | bytes 1572868

commit v4 on v3

--- a/solution.py
+++ b/solution.py
@@ -9,7 +9,7 @@
 from jax.experimental.pallas import tpu as pltpu
 from jax.sharding import PartitionSpec as P
 
-UNROLL = 16
+UNROLL = 32
 VMEM_LIMIT = 24 * 2**20
 GRID = 65536
 S = 32

time: 48.4 us -> 48.2 us (level)
  no operation moved by 1% of the time
where the time goes in v4:
time: 48.2 us; the launch traced here: 48.1 us
  Pallas kernels  45.7 us (95%)
  local copies, waits for them, and re-layouts  2.27 us (5%)
    pallas_call x1, Pallas kernels, gather_rows(): pl.pallas_call(functools.partial(rows_kernel, facets, times), out_shape=j...  26.6 us
    pallas_call x1, Pallas kernels, sum_facet(): pl.pallas_call(functools.partial(sum_kernel, scale, times), out_shape=jax...  15.5 us
    pallas_call x1, Pallas kernels, fold_facet(): pl.pallas_call(fold_kernel, out_shape=jax.ShapeDtypeStruct((2 * FP, FP),...  3.48 us
    unnamed x20, local copies, waits for them, and re-layouts  2.25 us

profile of v4, /device:TPU:1, one launch (start us, length us, event | category | flops | bytes accessed | tf_op | source)
XLA Modules:
  0.0 48.1 jit_solution(9408201300755466591)
XLA Ops:
  0.0 0.0 copy-start
  0.0 0.9 %copy-done = bf16[2,16,2,1024]{3,2,1,0:T(2,128)(2,1)S(1)} copy-done((bf16[2,16,2,1024]{3,2,1,0:T(2,128)(2,1)S(1)}, bf16[2,16,2,1024]{3,2,1,0:T(2,128)(2,1)}, u32[]{:S(2)}) %copy-start) | copy-done | bytes 131096
  0.9 0.0 copy-start.6
  0.9 0.0 copy-start.7
  1.0 0.0 copy-start.8
  1.0 0.7 %copy-done.6 = bf16[3,16,128]{2,1,0:T(8,128)(2,1)S(1)} copy-done((bf16[3,16,128]{2,1,0:T(8,128)(2,1)S(1)}, bf16[3,16,128]{2,1,0:T(8,128)(2,1)}, u32[]{:S(2)}) %copy-start.6) | copy-done | bytes 12312
  1.6 0.0 copy-done.7
  1.6 0.0 copy-done.8
  1.6 0.0 copy-start.1
  1.6 0.0 copy-start.4
  1.6 0.0 copy-start.5
  1.7 26.6 %subgrid_rows.1.mixed_ref = bf16[8,128,256]{2,1,0:T(8,128)(2,1)S(1)} custom-call(bf16[2,16,128]{2,1,0:T(8,128)(2,1)S(1)} %copy-done.7, bf16[3,16,128]{2,1,0:T(8,128)(2,1)S(1)} %copy-done.6, bf16[2,2,16,128]{3,2,1,0:T(8,128)(2,1)S(1)} %bitcast.11, s32[2,128]{1,0:T(2,128)S(1)} %bitcast.15), custom_call_target="tpu_custom_call" | custom-call | flops 2000000000 | bytes 10000000 | tf_op jit(solution)/shard_map/subgrid_rows/pallas_call | solution.py:292
  28.3 0.0 copy-done.1
  28.3 0.0 copy-done.4
  28.3 0.0 copy-done.5
  28.3 0.0 copy-start.2
  28.4 0.0 copy-start.3
  28.4 3.5 %fold_facet.1.folded_ref = bf16[1024,512]{1,0:T(8,128)(2,1)S(1)} custom-call(s32[1]{0:T(128)} %bitcast.facet_ref, s32[2,128]{1,0:T(2,128)S(1)} %bitcast.12, s32[2,128]{1,0:T(2,128)S(1)} %bitcast.13, s32[1,128]{1,0:T(1,128)S(1)} %bitcast.14, bf16[8,128,256]{2,1,0:T(8,128)(2,1)S(1)} %subgrid_rows.1.mixed_ref, bf16[8,256,256]{2,1,0:T(8,128)(2,1)S(1)} %copy-done.1), custom_call_target="tpu_custom_call" | custom-call | tf_op jit(solution)/shard_map/fold_facet/pallas_call | solution.py:450
  31.9 0.0 copy-done.2
  31.9 0.0 copy-done.3
  31.9 15.5 %sum_facet.1 = f32[2,16,512]{2,1,0:T(8,128)S(1)} custom-call(bf16[1024,512]{1,0:T(8,128)(2,1)S(1)} %fold_facet.1.folded_ref, bf16[4,256,256]{2,1,0:T(8,128)(2,1)S(1)} %copy-done.3, bf16[512,1024]{1,0:T(8,128)(2,1)S(1)} %copy-done.2), custom_call_target="tpu_custom_call" | custom-call | tf_op jit(solution)/shard_map/sum_facet/pallas_call | solution.py:602
  47.4 0.6 %copy.16 = f32[2,1,16,512]{3,2,1,0:T(8,128)} copy(f32[2,1,16,512]{3,2,1,0:T(8,128)S(1)} %bitcast.10) | data formatting | bytes 131072
  (2 shorter events, 0.0 us)
Async XLA Ops:
  0.0 0.9 %copy-start = (bf16[2,16,2,1024]{3,2,1,0:T(2,128)(2,1)S(1)}, bf16[2,16,2,1024]{3,2,1,0:T(2,128)(2,1)}, u32[]{:S(2)}) copy-start(bf16[2,16,2,1024]{3,2,1,0:T(2,128)(2,1)} %param.11) | copy-start | bytes 393220
  0.9 0.7 %copy-start.6 = (bf16[3,16,128]{2,1,0:T(8,128)(2,1)S(1)}, bf16[3,16,128]{2,1,0:T(8,128)(2,1)}, u32[]{:S(2)}) copy-start(bf16[3,16,128]{2,1,0:T(8,128)(2,1)} %coord_ref.1) | copy-start | bytes 36868
  0.9 0.7 %copy-start.7 = (bf16[2,16,128]{2,1,0:T(8,128)(2,1)S(1)}, bf16[2,16,128]{2,1,0:T(8,128)(2,1)}, u32[]{:S(2)}) copy-start(bf16[2,16,128]{2,1,0:T(8,128)(2,1)} %vis_ref.1) | copy-start | bytes 24580
  1.0 0.7 %copy-start.8 = (s32[128,2]{0,1:T(2,128)S(1)}, s32[128,2]{0,1:T(2,128)}, u32[]{:S(2)}) copy-start(s32[128,2]{0,1:T(2,128)} %param.12) | copy-start | bytes 3076
  1.6 26.7 %copy-start.1 = (bf16[8,256,256]{2,1,0:T(8,128)(2,1)S(1)}, bf16[8,256,256]{2,1,0:T(8,128)(2,1)}, u32[]{:S(2)}) copy-start(bf16[8,256,256]{2,1,0:T(8,128)(2,1)} %constant.18.clone.columns_ref) | copy-start | bytes 3145732
  1.6 26.7 %copy-start.4 = (s32[128,2]{0,1:T(2,128)S(1)}, s32[128,2]{0,1:T(2,128)}, u32[]{:S(2)}) copy-start(s32[128,2]{0,1:T(2,128)} %param.13) | copy-start | bytes 3076
  1.6 26.7 %copy-start.5 = (s32[128,1]{0,1:T(1,128)S(1)}, s32[128,1]{0,1:T(1,128)}, u32[]{:S(2)}) copy-start(s32[128,1]{0,1:T(1,128)} %param.14) | copy-start | bytes 1540
  28.3 3.5 %copy-start.2 = (bf16[512,1024]{1,0:T(8,128)(2,1)S(1)}, bf16[512,1024]{1,0:T(8,128)(2,1)}, u32[]{:S(2)}) copy-start(bf16[512,1024]{1,0:T(8,128)(2,1)} %constant.20.clone.edge_ref) | copy-start | bytes 3145732
  28.4 3.5 %copy-start.3 = (bf16[4,256,256]{2,1,0:T(8,128)(2,1)S(1)}, bf16[4,256,256]{2,1,0:T(8,128)(2,1)}, u32[]{:S(2)}) copy-start(bf16[4,256,256]{2,1,0:T(8,128)(2,1)} %constant.19.clone.rows_ref) | copy-start | bytes 1572868
